TPU v7x, 128 devices: a whole 4x4x4 slice. The times are simulated.
128 devices in a mesh: mem: 8 (over y, core), tile: 16 (over z, x).
Axes of the slice: x: 4, y: 4, z: 4, core: 2. Of those that a mesh axis runs over, the one named last changes fastest.
Arguments:
- solution: float32 [40, 4, 128, 1440], P('mem', None, 'tile'), may hold values from -6 to 6
- residual: float32 [40, 4, 128, 1440], P('mem', None, 'tile')
- direction: float32 [40, 4, 128, 1440], P('mem', None, 'tile')
- ensemble: bfloat16 [40, 4, 128, 1440], P('mem', None, 'tile'), may hold values from -6 to 6
- east_rate: float32 [128, 1440], P('tile'), may hold values from 0.06 to 0.12
- north_rate: float32 [128, 1440], P('tile'), may hold values from 0.18 to 0.36
- sea_mask: int32 [128, 1440], P('tile'), may hold values 0 or 1
- pass_counts: int32 [4], replicated, may hold values from 1 to 4, as said below
- obs_owner: int32 [131072, 1], P(('mem', 'tile')), may hold values from 0 to 127; in each aligned block of 1024 rows (0 to 1023, 1024 to 2047, ...) at most 16 rows name the same one
- obs_cell: int32 [131072], P(('mem', 'tile')), may hold values from 0 to 1439
- obs_level: int32 [131072], P(('mem', 'tile')), may hold values from 0 to 1
- obs_variable: int32 [131072], P(('mem', 'tile')), may hold values from 0 to 1
- obs_error: float32 [131072], P(('mem', 'tile')), may hold values from 0.5 to 2
Outputs:
- updated_solution: float32 [40, 4, 128, 1440], P('mem', None, 'tile')
- updated_residual: float32 [40, 4, 128, 1440], P('mem', None, 'tile')
Inputs may be any that keep to these rules, and one draw needn't show every extreme that they name: `pass_counts`: each field takes 1 to 4 passes; some field takes 4 and some field takes 1. `obs_owner`: owners are numbered d = (index along mem) * 16 + (index along tile) of the block of rows and longitudes they hold; the observations of one track segment name one owner at most 16 times, a bound that some block reaches. `obs_cell`: row within the band times 180 plus longitude within the block.
All inputs are finite; a program needn't handle non-finite values. No bound on the sum of `sea_mask` on one device may be relied on, other than what follows from the above.
Results may differ from a plain program's by a relative error of at most 0.0011.
Values may be sent and summed in bfloat16 or wider, within the bound.
A program may use at most 128 MiB of HBM per device.

v0:
```python
import math
import jax
import jax.numpy as jnp
from jax import lax
from jax.sharding import PartitionSpec as P

LEVELS = 2
PASSES = 4
ITERS = 2
CORRELATION = 0.6


def with_halo(block, sides, width):
    for axis, dim in sides:
        count = lax.axis_size(axis)
        forward = [(i, i + 1) for i in range(count - 1)]
        backward = [(target, source) for source, target in forward]
        low = lax.ppermute(
            lax.slice_in_dim(block, block.shape[dim] - width, None, axis=dim), axis, forward
        )
        high = lax.ppermute(lax.slice_in_dim(block, 0, width, axis=dim), axis, backward)
        block = jnp.concatenate([low, block, high], axis=dim)
    return block


def flow_step(padded, east_faces, north_faces):
    flux_north = north_faces * (padded[..., 1:, :] - padded[..., :-1, :])
    inner = padded[..., 1:-1, :]
    flux_east = east_faces * (jnp.roll(inner, -1, -1) - inner)
    return (
        inner
        + flux_east
        - jnp.roll(flux_east, 1, -1)
        + flux_north[..., 1:, :]
        - flux_north[..., :-1, :]
    )


def coefficients(east_rate, north_rate, sea_mask):
    margin = 1
    stacked = jnp.stack([east_rate, north_rate, sea_mask.astype(jnp.float32)])
    extended = with_halo(stacked, (("tile", 1),), margin)
    east_ext, north_ext, sea_ext = (extended[0], extended[1], extended[2])
    east_all = east_ext * sea_ext * jnp.roll(sea_ext, -1, 1)
    north_all = north_ext[:-1] * sea_ext[:-1] * sea_ext[1:]
    return (east_all, north_all, sea_ext, margin)


def smooth(field, coeffs, pass_counts):
    east_all, north_all, sea_ext, margin = coeffs
    band_rows = field.shape[2]
    sea_rows = sea_ext[margin : margin + band_rows]
    active = field * sea_rows
    applies = pass_counts[:, None, None]
    east_faces = east_all[margin : margin + band_rows]
    for sweep in range(PASSES):
        padded = with_halo(active, (("tile", 2),), 1)
        moved = flow_step(padded, east_faces, north_all)
        active = jnp.where(sweep < applies, moved, active)
    return active * sea_rows


def precision_apply(values, errors):
    scaled = values / errors
    length = scaled.shape[0]
    zero_col = jnp.zeros((1,), jnp.float32)
    following = jnp.concatenate([scaled[1:], zero_col])
    preceding = jnp.concatenate([zero_col, scaled[:-1]])
    position = jnp.arange(length, dtype=jnp.int32)
    at_ends = ((position == 0) | (position == length - 1)).astype(jnp.float32)
    diagonal = 1.0 + CORRELATION * CORRELATION - CORRELATION * CORRELATION * at_ends
    mixed = (diagonal * scaled - CORRELATION * (following + preceding)) / (
        1.0 - CORRELATION * CORRELATION
    )
    return mixed / errors


def shards(
    solution,
    residual,
    direction,
    ensemble,
    east_rate,
    north_rate,
    sea_mask,
    pass_counts,
    obs_owner,
    obs_cell,
    obs_level,
    obs_variable,
    obs_error,
):
    coeffs = coefficients(east_rate, north_rate, sea_mask)
    mem_count = lax.axis_size("mem")
    devices = mem_count * lax.axis_size("tile")
    weight = 1.0 / math.sqrt(ensemble.shape[0] * mem_count - 1)
    band_rows = solution.shape[2]
    block_cols = solution.shape[3] // mem_count
    owners = obs_owner[:, 0]
    segment = owners.shape[0]
    capacity = 2 * segment // devices
    one_hot = (owners[:, None] == jnp.arange(devices, dtype=jnp.int32)[None, :]).astype(jnp.int32)
    slot_index = jnp.sum(one_hot * (jnp.cumsum(one_hot, 0) - 1), 1)
    cell_index = (obs_variable * LEVELS + obs_level) * (band_rows * block_cols) + obs_cell
    send_ids = jnp.zeros((devices, capacity), jnp.int32).at[owners, slot_index].set(cell_index)
    wanted = lax.all_to_all(
        send_ids, ("mem", "tile"), split_axis=0, concat_axis=0, tiled=True
    ).reshape(-1)
    tiled_pert = lax.all_to_all(ensemble, "mem", split_axis=3, concat_axis=0, tiled=True)

    def global_sum(value):
        return lax.psum(value, ("mem", "tile"))

    norm_now = global_sum(jnp.sum(residual * residual))
    for iteration in range(ITERS):
        shaped = smooth(direction, coeffs, pass_counts).astype(jnp.bfloat16)
        gathered = lax.all_to_all(shaped, "mem", split_axis=3, concat_axis=0, tiled=True)
        increment = (
            jnp.sum(tiled_pert.astype(jnp.float32) * gathered.astype(jnp.float32), 0) * weight
        )
        picked = increment.reshape(-1)[wanted].reshape(devices, capacity)
        returned = lax.all_to_all(picked, ("mem", "tile"), split_axis=0, concat_axis=0, tiled=True)
        obs_value = returned[owners, slot_index]
        weighted = precision_apply(obs_value, obs_error)
        outgoing = jnp.zeros((devices, capacity), jnp.float32).at[owners, slot_index].set(weighted)
        arrived = lax.all_to_all(outgoing, ("mem", "tile"), split_axis=0, concat_axis=0, tiled=True)
        adjoint = (
            jnp.zeros((increment.size,), jnp.float32)
            .at[wanted]
            .add(arrived.reshape(-1))
            .reshape(increment.shape)
        )
        spread = (tiled_pert.astype(jnp.float32) * adjoint[None] * weight).astype(jnp.bfloat16)
        back = lax.all_to_all(spread, "mem", split_axis=0, concat_axis=3, tiled=True)
        image = direction + smooth(back.astype(jnp.float32), coeffs, pass_counts)
        step_size = norm_now / global_sum(jnp.sum(direction * image))
        solution = solution + step_size * direction
        residual = residual - step_size * image
        if iteration + 1 < ITERS:
            norm_next = global_sum(jnp.sum(residual * residual))
            direction = residual + norm_next / norm_now * direction
            norm_now = norm_next
    return (solution, residual)


def solution(mesh):
    return jax.shard_map(
        shards,
        mesh=mesh,
        in_specs=(
            P("mem", None, "tile", None),
            P("mem", None, "tile", None),
            P("mem", None, "tile", None),
            P("mem", None, "tile", None),
            P("tile", None),
            P("tile", None),
            P("tile", None),
            P(),
            P(("mem", "tile"), None),
            P(("mem", "tile")),
            P(("mem", "tile")),
            P(("mem", "tile")),
            P(("mem", "tile")),
        ),
        out_specs=(P("mem", None, "tile", None), P("mem", None, "tile", None)),
        check_vma=False,
    )
```

profile of v0, /device:TPU:1, one launch (start us, length us, event | category | flops | bytes accessed | tf_op | source)
XLA Modules:
  0.0 769.5 jit_solution(7420119793603275000)
XLA Ops:
  2.7 4.3 scatter_custom_fusion.2
  7.8 11.5 %all-to-all-start.1 = ((s32[128,1,16]{2,1,0:T(1,128)}), s32[128,1,16]{2,1,0:T(1,128)S(1)}, u32[]{:S(2)}, u32[]{:S(2)}) async-start(s32[128,1,16]{2,1,0:T(1,128)} %copy.101), calls=%async_computation.1 | async-start | bytes 131072 | tf_op jit(solution)/shard_map/all_to_all | solution.py:106
  21.5 4.6 collective-permute-start.3
  33.4 16.8 %copy.96 = bf16[5,4,8,1440]{2,0,1,3:T(8,128)(2,1)} copy(bf16[5,4,8,1440]{3,2,1,0:T(8,128)(2,1)S(1)} %copy-done.10) | data formatting | bytes 921600 | tf_op args[3]
  50.2 11.8 %reshape.273 = bf16[8,2,14400]{2,1,0:T(2,128)(2,1)} reshape(bf16[1440,4,5,8]{3,2,1,0:T(8,128)(2,1)} %bitcast.97) | data formatting | bytes 921600
  62.0 6.3 all-to-all-start
  85.0 4.7 collective-permute-start.7
  94.3 6.1 collective-permute-start.9
  103.2 7.1 copy.102
  110.3 10.5 %reshape.275 = bf16[8,2,14400]{2,1,0:T(2,128)(2,1)} reshape(bf16[1440,5,4,8]{3,2,1,0:T(4,128)(2,1)} %bitcast.98) | data formatting | bytes 921600
  120.8 7.0 all-to-all-start.2
  127.8 10.9 %reshape.274 = bf16[1440,4,5,8]{3,2,1,0:T(8,128)(2,1)} reshape(bf16[8,2,14400]{2,1,0:T(2,128)(2,1)} %all-to-all-done) | data formatting | bytes 921600
  138.7 10.8 %copy.97 = bf16[5,4,8,1440]{3,2,1,0:T(8,128)(2,1)S(1)} copy(bf16[5,4,8,1440]{2,0,1,3:T(8,128)(2,1)} %bitcast.96) | data formatting | bytes 921600 | tf_op jit(solution)/shard_map/all_to_all | solution.py:109
  149.5 7.5 reshape.276
  157.0 8.6 %copy.103 = bf16[5,4,8,1440]{3,2,1,0:T(8,128)(2,1)S(1)} copy(bf16[5,4,8,1440]{2,1,0,3:T(4,128)(2,1)} %bitcast.99) | data formatting | bytes 921600 | tf_op jit(solution)/shard_map/all_to_all | solution.py:117
  171.2 11.8 %gather_fusion = f32[2048]{0:T(1024)S(1)} fusion(f32[5760]{0:T(1024)S(1)} %mul.420, s32[2048]{0:T(1024)S(1)} %broadcast_clamp_fusion), kind=kCustom, calls=%fused_computation | custom fusion | bytes 24576 | tf_op jit(solution)/shard_map/gather | solution.py:121
  183.1 28.9 %all_to_all.96 = f32[128,1,16]{2,1,0:T(1,128)S(1)} all-to-all(f32[128,1,16]{2,1,0:T(1,128)S(1)} %bitcast.128), channel_id=1, replica_groups=mesh['mem'=8,'tile'=16] {'mem','tile'}, dimensions={0} | all-to-all | bytes 16384 | tf_op jit(solution)/shard_map/all_to_all | solution.py:122
  212.0 7.1 gather_fusion.1
  219.3 4.4 scatter_custom_fusion.3
  224.5 4.8 all-to-all-start.4
  233.1 6.0 all-to-all-done.4
  241.9 12.9 %scatter_custom_fusion = f32[5760]{0:T(1024)S(1)} fusion(s32[2048]{0:T(1024)} %bitcast.136, f32[2048]{0:T(1024)S(1)} %reshape.208, f32[]{:T(128)} %constant.17.clone.1), kind=kCustom, calls=%fused_computation.204 | custom fusion | flops 2048 | bytes 23552 | tf_op jit(solution)/shard_map/scatter-add | solution.py:130
  256.0 5.0 all-to-all-start.5
  261.9 10.0 %all-to-all-done.5 = bf16[40,4,8,180]{3,2,1,0:T(8,128)(2,1)} async-done(((bf16[40,4,8,180]{3,2,1,0:T(8,128)(2,1)}), bf16[40,4,8,180]{3,2,1,0:T(8,128)(2,1)}, u32[]{:S(2)}, u32[]{:S(2)}) %all-to-all-start.5) | async-done | bytes 460832 | tf_op jit(solution)/shard_map/all_to_all | solution.py:134
  287.5 4.4 collective-permute-start.13
  296.6 4.7 collective-permute-start.15
  306.0 4.4 collective-permute-start.17
  314.9 76.2 %all-reduce = (f32[]{:T(128)}, f32[]{:T(128)}) all-reduce(f32[]{:T(128)} %multiply_reduce_fusion.5, f32[]{:T(128)} %get-tuple-element.10), channel_id=1, replica_groups=mesh['mem'=8,'tile'=16] {'mem','tile'}, use_global_device_ids=true, to_apply=%region_1.2 | all-reduce | flops 2 | bytes 16 | tf_op jit(solution)/shard_map/psum | solution.py:112
  394.9 63.1 %psum.30 = f32[]{:T(128)} all-reduce(f32[]{:T(128)} %get-tuple-element.8), channel_id=1, replica_groups=mesh['mem'=8,'tile'=16] {'mem','tile'}, use_global_device_ids=true, to_apply=%region_13.14 | all-reduce | flops 1 | bytes 8 | tf_op jit(solution)/shard_map/psum | solution.py:112
  470.8 4.4 collective-permute-start.21
  479.8 4.7 collective-permute-start.23
  489.1 4.4 collective-permute-start.25
  497.2 8.8 %copy.109 = bf16[5,4,8,1440]{2,1,0,3:T(4,128)(2,1)} copy(bf16[5,4,8,1440]{3,2,1,0:T(8,128)(2,1)} %fusion.28) | data formatting | bytes 921600 | tf_op jit(solution)/shard_map/convert_element_type | solution.py:116
  506.0 9.8 %reshape.277 = bf16[8,2,14400]{2,1,0:T(2,128)(2,1)S(1)} reshape(bf16[1440,5,4,8]{3,2,1,0:T(4,128)(2,1)} %bitcast.100) | data formatting | bytes 921600
  515.8 17.0 %all_to_all.97 = bf16[8,2,14400]{2,1,0:T(2,128)(2,1)S(1)} all-to-all(bf16[8,2,14400]{2,1,0:T(2,128)(2,1)S(1)} %reshape.277), channel_id=1, replica_groups=mesh['mem'=8,'tile'=16] {'mem'}, dimensions={0} | all-to-all | bytes 921600 | tf_op jit(solution)/shard_map/all_to_all | solution.py:117
  532.8 7.5 reshape.278
  540.2 8.6 %copy.110 = bf16[5,4,8,1440]{3,2,1,0:T(8,128)(2,1)S(1)} copy(bf16[5,4,8,1440]{2,1,0,3:T(4,128)(2,1)} %bitcast.101) | data formatting | bytes 921600 | tf_op jit(solution)/shard_map/all_to_all | solution.py:117
  556.0 11.8 %gather_fusion.2 = f32[2048]{0:T(1024)S(1)} fusion(f32[5760]{0:T(1024)S(1)} %mul.456, s32[2048]{0:T(1024)S(1)} %broadcast_clamp_fusion), kind=kCustom, calls=%fused_computation.2 | custom fusion | bytes 24576 | tf_op jit(solution)/shard_map/gather | solution.py:121
  567.9 24.4 %all_to_all.98 = f32[128,1,16]{2,1,0:T(1,128)S(1)} all-to-all(f32[128,1,16]{2,1,0:T(1,128)S(1)} %bitcast.129), channel_id=1, replica_groups=mesh['mem'=8,'tile'=16] {'mem','tile'}, dimensions={0} | all-to-all | bytes 16384 | tf_op jit(solution)/shard_map/all_to_all | solution.py:122
  592.3 7.1 gather_fusion.3
  599.5 4.4 scatter_custom_fusion.4
  604.1 13.9 %all_to_all.99 = f32[128,1,16]{2,1,0:T(1,128)S(1)} all-to-all(f32[128,1,16]{2,1,0:T(1,128)S(1)} %copy.114), channel_id=1, replica_groups=mesh['mem'=8,'tile'=16] {'mem','tile'}, dimensions={0} | all-to-all | bytes 16384 | tf_op jit(solution)/shard_map/all_to_all | solution.py:126
  618.9 12.9 %scatter_custom_fusion.1 = f32[5760]{0:T(1024)S(1)} fusion(s32[2048]{0:T(1024)} %bitcast.137, f32[2048]{0:T(1024)S(1)} %reshape.216, f32[]{:T(128)} %constant.17.clone.1), kind=kCustom, calls=%fused_computation.202 | custom fusion | flops 2048 | bytes 23552 | tf_op jit(solution)/shard_map/scatter-add | solution.py:130
  632.1 14.2 %all_to_all.100 = bf16[40,4,8,180]{3,2,1,0:T(8,128)(2,1)S(1)} all-to-all(bf16[40,4,8,180]{3,2,1,0:T(8,128)(2,1)S(1)} %fusion.19), channel_id=1, replica_groups=mesh['mem'=8,'tile'=16] {'mem'}, dimensions={0} | all-to-all | bytes 921600 | tf_op jit(solution)/shard_map/all_to_all | solution.py:134
  660.9 4.7 collective-permute-start.29
  669.9 4.7 collective-permute-start.31
  679.3 4.4 collective-permute-start.33
  688.2 75.9 %psum.31 = f32[]{:T(128)} all-reduce(f32[]{:T(128)} %get-tuple-element.4), channel_id=1, replica_groups=mesh['mem'=8,'tile'=16] {'mem','tile'}, use_global_device_ids=true, to_apply=%region_19.20 | all-reduce | flops 1 | bytes 8 | tf_op jit(solution)/shard_map/psum | solution.py:112
  (321 shorter events, 147.1 us)
Async XLA Ops:
  2.0 24.2 %copy-start.11 = (f32[8,1440]{1,0:T(8,128)S(1)}, f32[8,1440]{1,0:T(8,128)}, u32[]{:S(2)}) copy-start(f32[8,1440]{1,0:T(8,128)} %param.18) | copy-start | bytes 138244
  2.0 24.2 %copy-start.12 = (f32[8,1440]{1,0:T(8,128)S(1)}, f32[8,1440]{1,0:T(8,128)}, u32[]{:S(2)}) copy-start(f32[8,1440]{1,0:T(8,128)} %param.17) | copy-start | bytes 138244
  2.0 29.5 %copy-start.35 = (s32[4]{0:T(128)S(1)}, s32[4]{0:T(128)}, u32[]{:S(2)}) copy-start(s32[4]{0:T(128)} %param.20) | copy-start | bytes 52
  7.8 54.2 %all-to-all-start.1 = ((s32[128,1,16]{2,1,0:T(1,128)}), s32[128,1,16]{2,1,0:T(1,128)S(1)}, u32[]{:S(2)}, u32[]{:S(2)}) async-start(s32[128,1,16]{2,1,0:T(1,128)} %copy.101), calls=%async_computation.1 | async-start | bytes 131072 | tf_op jit(solution)/shard_map/all_to_all | solution.py:106
  19.4 30.8 %copy-start.1 = (f32[5,4,8,1440]{3,2,1,0:T(8,128)}, f32[5,4,8,1440]{3,2,1,0:T(8,128)S(1)}, u32[]{:S(2)}) copy-start(f32[5,4,8,1440]{3,2,1,0:T(8,128)S(1)} %broadcast_multiply_fusion.3) | copy-start | bytes 2764804
  20.3 51.9 %collective-permute-start.2 = (f32[5,4,1,1440]{3,2,1,0:T(1,128)}, f32[5,4,1,1440]{3,2,1,0:T(1,128)}, u32[]{:S(2)}, u32[]{:S(2)}) collective-permute-start(f32[5,4,1,1440]{3,2,1,0:T(1,128)} %get-tuple-element.43), channel_id=1, source_target_pairs={{1,0},{2,1},{3,2},{4,3},{5,4},{6,5},{7,6},{8,7},{9,8},{10,9},{11,1... | collective-permute-start | bytes 345608 | tf_op jit(solution)/shard_map/ppermute | solution.py:21
  21.5 50.6 %collective-permute-start.3 = (f32[5,4,1,1440]{3,2,1,0:T(1,128)}, f32[5,4,1,1440]{3,2,1,0:T(1,128)}, u32[]{:S(2)}, u32[]{:S(2)}) collective-permute-start(f32[5,4,1,1440]{3,2,1,0:T(1,128)} %get-tuple-element.42), channel_id=1, source_target_pairs={{0,1},{1,2},{2,3},{3,4},{4,5},{5,6},{6,7},{7,8},{8,9},{9,10},{10,1... | collective-permute-start | bytes 345608 | tf_op jit(solution)/shard_map/ppermute | solution.py:18
  26.2 43.5 %collective-permute-start.1 = (f32[3,1,1440]{2,1,0:T(1,128)S(1)}, f32[3,1,1440]{2,1,0:T(1,128)S(1)}, u32[]{:S(2)}, u32[]{:S(2)}) collective-permute-start(f32[3,1,1440]{2,1,0:T(1,128)S(1)} %get-tuple-element.47), channel_id=1, source_target_pairs={{1,0},{2,1},{3,2},{4,3},{5,4},{6,5},{7,6},{8,7},{9,8},{10,9},{11,1... | collective-permute-start | bytes 51848 | tf_op jit(solution)/shard_map/ppermute | solution.py:21
  27.5 42.2 %collective-permute-start = (f32[3,1,1440]{2,1,0:T(1,128)S(1)}, f32[3,1,1440]{2,1,0:T(1,128)S(1)}, u32[]{:S(2)}, u32[]{:S(2)}) collective-permute-start(f32[3,1,1440]{2,1,0:T(1,128)S(1)} %get-tuple-element.46), channel_id=1, source_target_pairs={{0,1},{1,2},{2,3},{3,4},{4,5},{5,6},{6,7},{7,8},{8,9},{9,10},{10,1... | collective-permute-start | bytes 51848 | tf_op jit(solution)/shard_map/ppermute | solution.py:18
  32.1 41.4 %copy-start.28 = (pred[4]{0:T(512)(128)(4,1)}, pred[4]{0:T(512)(128)(4,1)S(1)}, u32[]{:S(2)}) copy-start(pred[4]{0:T(512)(128)(4,1)S(1)} %get-tuple-element.59) | copy-start | bytes 16
  32.1 70.4 %copy-start.19 = (pred[4]{0:T(512)(128)(4,1)}, pred[4]{0:T(512)(128)(4,1)S(1)}, u32[]{:S(2)}) copy-start(pred[4]{0:T(512)(128)(4,1)S(1)} %get-tuple-element.57) | copy-start | bytes 16
  62.0 58.9 %all-to-all-start = ((bf16[8,2,14400]{2,1,0:T(2,128)(2,1)}), bf16[8,2,14400]{2,1,0:T(2,128)(2,1)}, u32[]{:S(2)}, u32[]{:S(2)}) async-start(bf16[8,2,14400]{2,1,0:T(2,128)(2,1)} %reshape.273), calls=%async_computation | async-start | bytes 925696 | tf_op jit(solution)/shard_map/all_to_all | solution.py:109
  74.7 6.6 collective-permute-start.4
  76.0 6.2 collective-permute-start.5
  83.7 6.4 collective-permute-start.6
  85.0 6.6 collective-permute-start.7
  93.0 7.7 %collective-permute-start.8 = (f32[5,4,1,1440]{3,2,1,0:T(1,128)S(1)}, f32[5,4,1,1440]{3,2,1,0:T(1,128)S(1)}, u32[]{:S(2)}, u32[]{:S(2)}) collective-permute-start(f32[5,4,1,1440]{3,2,1,0:T(1,128)S(1)} %get-tuple-element.37), channel_id=1, source_target_pairs={{1,0},{2,1},{3,2},{4,3},{5,4},{6,5},{7,6},{8,7},{9,8},{10,9},{11,1... | collective-permute-start | bytes 345608 | tf_op jit(solution)/shard_map/ppermute | solution.py:21
  94.3 7.8 %collective-permute-start.9 = (f32[5,4,1,1440]{3,2,1,0:T(1,128)S(1)}, f32[5,4,1,1440]{3,2,1,0:T(1,128)S(1)}, u32[]{:S(2)}, u32[]{:S(2)}) collective-permute-start(f32[5,4,1,1440]{3,2,1,0:T(1,128)S(1)} %get-tuple-element.36), channel_id=1, source_target_pairs={{0,1},{1,2},{2,3},{3,4},{4,5},{5,6},{6,7},{7,8},{8,9},{9,10},{10,1... | collective-permute-start | bytes 345608 | tf_op jit(solution)/shard_map/ppermute | solution.py:18
  120.8 28.7 %all-to-all-start.2 = ((bf16[8,2,14400]{2,1,0:T(2,128)(2,1)}), bf16[8,2,14400]{2,1,0:T(2,128)(2,1)S(1)}, u32[]{:S(2)}, u32[]{:S(2)}) async-start(bf16[8,2,14400]{2,1,0:T(2,128)(2,1)} %reshape.275), calls=%async_computation.2 | async-start | bytes 925696 | tf_op jit(solution)/shard_map/all_to_all | solution.py:117
  149.5 79.8 %copy-start.6 = (bf16[5,4,8,1440]{3,2,1,0:T(8,128)(2,1)}, bf16[5,4,8,1440]{3,2,1,0:T(8,128)(2,1)S(1)}, u32[]{:S(2)}) copy-start(bf16[5,4,8,1440]{3,2,1,0:T(8,128)(2,1)S(1)} %copy.97) | copy-start | bytes 1382404
  224.5 14.6 %all-to-all-start.4 = ((f32[128,1,16]{2,1,0:T(1,128)}), f32[128,1,16]{2,1,0:T(1,128)S(1)}, u32[]{:S(2)}, u32[]{:S(2)}) async-start(f32[128,1,16]{2,1,0:T(1,128)} %copy.107), calls=%async_computation.4 | async-start | bytes 131072 | tf_op jit(solution)/shard_map/all_to_all | solution.py:126
  233.0 27.9 %copy-start.9 = (f32[5,4,8,1440]{3,2,1,0:T(8,128)S(1)}, f32[5,4,8,1440]{3,2,1,0:T(8,128)}, u32[]{:S(2)}) copy-start(f32[5,4,8,1440]{3,2,1,0:T(8,128)} %param.14) | copy-start | bytes 2764804
  256.0 15.9 %all-to-all-start.5 = ((bf16[40,4,8,180]{3,2,1,0:T(8,128)(2,1)}), bf16[40,4,8,180]{3,2,1,0:T(8,128)(2,1)}, u32[]{:S(2)}, u32[]{:S(2)}) async-start(bf16[40,4,8,180]{3,2,1,0:T(8,128)(2,1)} %fusion.17), calls=%async_computation.5 | async-start | bytes 1310720 | tf_op jit(solution)/shard_map/all_to_all | solution.py:134
  277.5 5.6 collective-permute-start.10
  278.8 5.8 collective-permute-start.11
  286.2 6.0 collective-permute-start.12
  287.5 6.3 collective-permute-start.13
  295.3 6.3 collective-permute-start.14
  296.6 6.5 collective-permute-start.15
  304.7 6.0 collective-permute-start.16
  306.0 6.3 collective-permute-start.17
  394.9 65.6 %copy-start.4 = (f32[5,4,8,1440]{3,2,1,0:T(8,128)}, f32[5,4,8,1440]{3,2,1,0:T(8,128)S(1)}, u32[]{:S(2)}) copy-start(f32[5,4,8,1440]{3,2,1,0:T(8,128)S(1)} %get-tuple-element.9) | copy-start | bytes 2764804
  460.9 6.1 collective-permute-start.18
  462.2 5.8 collective-permute-start.19
  469.5 6.0 collective-permute-start.20
  470.8 6.3 collective-permute-start.21
  478.5 6.3 collective-permute-start.22
  479.8 6.5 collective-permute-start.23
  487.8 6.0 collective-permute-start.24
  489.1 6.3 collective-permute-start.25
  650.9 5.6 collective-permute-start.26
  652.2 5.8 collective-permute-start.27
  659.6 6.3 collective-permute-start.28
  660.9 6.3 collective-permute-start.29
  668.6 6.3 collective-permute-start.30
  669.9 6.5 collective-permute-start.31
  678.0 6.0 collective-permute-start.32
  679.3 6.3 collective-permute-start.33
  (30 other events, 134.2 us)
where the time goes:
time: 782 us; the launch traced here: 770 us
  blocking collectives  314 us (40%)
  local copies, waits for them, and re-layouts  204 us (26%)
  starting transfers between devices  133 us (17%)
  other arithmetic  73.2 us (9%)
  waiting for transfers between devices  39.1 us (5%)
    psum x3, blocking collectives, global_sum(): return lax.psum(value, ('mem', 'tile'))  215 us
    unnamed x88, local copies, waits for them, and re-layouts  94.7 us
    ppermute x17, starting transfers between devices, with_halo(): lax.ppermute(lax.slice_in_dim(block, block.shape[dim] - width, None, axis...  76.2 us
    all_to_all x2, blocking collectives, shards(): lax.all_to_all(picked, ('mem', 'tile'), split_axis=0, concat_axis=0, tile...  53.3 us
    scatter-add x2, other arithmetic, shards(): adjoint = jnp.zeros((increment.size,), jnp.float32).at[wanted].add(arrive...  25.9 us
    gather x2, local copies, waits for them, and re-layouts, shards(): picked = increment.reshape(-1)[wanted].reshape(devices, capacity)  23.6 us
    ppermute x17, starting transfers between devices, with_halo(): lax.ppermute(lax.slice_in_dim(block, 0, width, axis=dim), axis, backward)  21.9 us
    ppermute x17, waiting for transfers between devices, with_halo(): lax.ppermute(lax.slice_in_dim(block, block.shape[dim] - width, None, axis...  21.3 us
  transfers between devices with their start and end apart: 39, of which 19 were waited for; matrix products, arithmetic and copies ran while one was open for 12% of the time, Pallas kernels for 0%

commit v1 on v0

--- a/solution.py
+++ b/solution.py
@@ -109,7 +109,7 @@
     tiled_pert = lax.all_to_all(ensemble, "mem", split_axis=3, concat_axis=0, tiled=True)
 
     def global_sum(value):
-        return lax.psum(value, ("mem", "tile"))
+        return lax.psum(lax.psum(value, "tile"), "mem")
 
     norm_now = global_sum(jnp.sum(residual * residual))
     for iteration in range(ITERS):

time: 782 us -> 737 us (0.942)
  blocking collectives: 314 us -> 268 us
    psum x3 -> x6, blocking collectives: 215 us -> 173 us  [global_sum(): return lax.psum(lax.psum(value, 'tile'), 'mem')]
where the time goes in v1:
time: 737 us; the launch traced here: 725 us
  blocking collectives  268 us (36%)
  local copies, waits for them, and re-layouts  204 us (28%)
  starting transfers between devices  134 us (18%)
  other arithmetic  73.2 us (10%)
  waiting for transfers between devices  39.3 us (5%)
    psum x6, blocking collectives, global_sum(): return lax.psum(lax.psum(value, 'tile'), 'mem')  173 us
    unnamed x88, local copies, waits for them, and re-layouts  94.6 us
    ppermute x17, starting transfers between devices, with_halo(): lax.ppermute(lax.slice_in_dim(block, block.shape[dim] - width, None, axis...  77 us
    all_to_all x2, blocking collectives, shards(): lax.all_to_all(picked, ('mem', 'tile'), split_axis=0, concat_axis=0, tile...  51.8 us
    scatter-add x2, other arithmetic, shards(): adjoint = jnp.zeros((increment.size,), jnp.float32).at[wanted].add(arrive...  25.9 us
    gather x2, local copies, waits for them, and re-layouts, shards(): picked = increment.reshape(-1)[wanted].reshape(devices, capacity)  23.6 us
    ppermute x17, starting transfers between devices, with_halo(): lax.ppermute(lax.slice_in_dim(block, 0, width, axis=dim), axis, backward)  21.9 us
    ppermute x17, waiting for transfers between devices, with_halo(): lax.ppermute(lax.slice_in_dim(block, block.shape[dim] - width, None, axis...  21.3 us
  transfers between devices with their start and end apart: 39, of which 19 were waited for; matrix products, arithmetic and copies ran while one was open for 12% of the time, Pallas kernels for 0%

profile of v1, /device:TPU:1, one launch (start us, length us, event | category | flops | bytes accessed | tf_op | source)
XLA Modules:
  0.0 724.7 jit_solution(3284905146288463926)
XLA Ops:
  7.7 11.5 %all-to-all-start.1 = ((s32[128,1,16]{2,1,0:T(1,128)}), s32[128,1,16]{2,1,0:T(1,128)S(1)}, u32[]{:S(2)}, u32[]{:S(2)}) async-start(s32[128,1,16]{2,1,0:T(1,128)} %copy.101), calls=%async_computation.1 | async-start | bytes 131072 | tf_op jit(solution)/shard_map/all_to_all | solution.py:106
  21.5 4.7 collective-permute-start.3
  33.3 16.8 %copy.96 = bf16[5,4,8,1440]{2,0,1,3:T(8,128)(2,1)} copy(bf16[5,4,8,1440]{3,2,1,0:T(8,128)(2,1)S(1)} %copy-done.10) | data formatting | bytes 921600 | tf_op args[3]
  50.1 11.8 %reshape.273 = bf16[8,2,14400]{2,1,0:T(2,128)(2,1)} reshape(bf16[1440,4,5,8]{3,2,1,0:T(8,128)(2,1)} %bitcast.97) | data formatting | bytes 921600
  61.9 6.3 all-to-all-start
  85.0 4.7 collective-permute-start.7
  94.4 6.1 collective-permute-start.9
  103.2 7.1 copy.102
  110.3 10.5 %reshape.275 = bf16[8,2,14400]{2,1,0:T(2,128)(2,1)} reshape(bf16[1440,5,4,8]{3,2,1,0:T(4,128)(2,1)} %bitcast.98) | data formatting | bytes 921600
  120.8 7.0 all-to-all-start.2
  127.8 10.8 %reshape.274 = bf16[1440,4,5,8]{3,2,1,0:T(8,128)(2,1)} reshape(bf16[8,2,14400]{2,1,0:T(2,128)(2,1)} %all-to-all-done) | data formatting | bytes 921600
  138.6 10.8 %copy.97 = bf16[5,4,8,1440]{3,2,1,0:T(8,128)(2,1)S(1)} copy(bf16[5,4,8,1440]{2,0,1,3:T(8,128)(2,1)} %bitcast.96) | data formatting | bytes 921600 | tf_op jit(solution)/shard_map/all_to_all | solution.py:109
  149.4 7.5 %reshape.276 = bf16[1440,5,4,8]{3,2,1,0:T(4,128)(2,1)} reshape(bf16[8,2,14400]{2,1,0:T(2,128)(2,1)S(1)} %all-to-all-done.2) | data formatting | bytes 921600
  156.9 8.6 %copy.103 = bf16[5,4,8,1440]{3,2,1,0:T(8,128)(2,1)S(1)} copy(bf16[5,4,8,1440]{2,1,0,3:T(4,128)(2,1)} %bitcast.99) | data formatting | bytes 921600 | tf_op jit(solution)/shard_map/all_to_all | solution.py:117
  171.2 11.8 %gather_fusion = f32[2048]{0:T(1024)S(1)} fusion(f32[5760]{0:T(1024)S(1)} %mul.420, s32[2048]{0:T(1024)S(1)} %broadcast_clamp_fusion), kind=kCustom, calls=%fused_computation | custom fusion | bytes 24576 | tf_op jit(solution)/shard_map/gather | solution.py:121
  183.0 28.9 %all_to_all.96 = f32[128,1,16]{2,1,0:T(1,128)S(1)} all-to-all(f32[128,1,16]{2,1,0:T(1,128)S(1)} %bitcast.128), channel_id=1, replica_groups=mesh['mem'=8,'tile'=16] {'mem','tile'}, dimensions={0} | all-to-all | bytes 16384 | tf_op jit(solution)/shard_map/all_to_all | solution.py:122
  212.0 7.1 gather_fusion.1
  219.2 4.4 scatter_custom_fusion.3
  224.4 4.8 all-to-all-start.4
  233.0 6.0 all-to-all-done.4
  241.8 12.9 %scatter_custom_fusion = f32[5760]{0:T(1024)S(1)} fusion(s32[2048]{0:T(1024)} %bitcast.136, f32[2048]{0:T(1024)S(1)} %reshape.208, f32[]{:T(128)} %constant.17.clone.1), kind=kCustom, calls=%fused_computation.204 | custom fusion | flops 2048 | bytes 23552 | tf_op jit(solution)/shard_map/scatter-add | solution.py:130
  255.9 5.0 all-to-all-start.5
  261.9 10.0 %all-to-all-done.5 = bf16[40,4,8,180]{3,2,1,0:T(8,128)(2,1)} async-done(((bf16[40,4,8,180]{3,2,1,0:T(8,128)(2,1)}), bf16[40,4,8,180]{3,2,1,0:T(8,128)(2,1)}, u32[]{:S(2)}, u32[]{:S(2)}) %all-to-all-start.5) | async-done | bytes 460832 | tf_op jit(solution)/shard_map/all_to_all | solution.py:134
  287.5 4.4 collective-permute-start.13
  296.5 4.7 collective-permute-start.15
  305.9 4.4 collective-permute-start.17
  314.8 36.4 %all-reduce = (f32[]{:T(128)}, f32[]{:T(128)}) all-reduce(f32[]{:T(128)} %multiply_reduce_fusion.5, f32[]{:T(128)} %get-tuple-element.12), channel_id=1, replica_groups=mesh['mem'=8,'tile'=16] {'tile'}, use_global_device_ids=true, to_apply=%region_1.2 | all-reduce | flops 2 | bytes 16 | tf_op jit(solution)/shard_map/psum | solution.py:112
  351.2 25.6 %all-reduce.1 = (f32[]{:T(128)}, f32[]{:T(128)}) all-reduce(f32[]{:T(128)} %get-tuple-element.2, f32[]{:T(128)} %get-tuple-element.3), channel_id=1, replica_groups=mesh['mem'=8,'tile'=16] {'mem'}, use_global_device_ids=true, to_apply=%region_2.3 | all-reduce | flops 2 | bytes 16 | tf_op jit(solution)/shard_map/psum | solution.py:112
  380.5 29.1 %psum.60 = f32[]{:T(128)} all-reduce(f32[]{:T(128)} %get-tuple-element.10), channel_id=1, replica_groups=mesh['mem'=8,'tile'=16] {'tile'}, use_global_device_ids=true, to_apply=%region_15.16 | all-reduce | flops 1 | bytes 8 | tf_op jit(solution)/shard_map/psum | solution.py:112
  409.6 20.1 %psum.61 = f32[]{:T(128)} all-reduce(f32[]{:T(128)} %psum.60), channel_id=1, replica_groups=mesh['mem'=8,'tile'=16] {'mem'}, use_global_device_ids=true, to_apply=%region_16.17 | all-reduce | flops 1 | bytes 8 | tf_op jit(solution)/shard_map/psum | solution.py:112
  442.8 4.9 collective-permute-start.21
  452.3 4.7 collective-permute-start.23
  461.6 4.7 collective-permute-start.25
  470.0 8.7 %copy.109 = bf16[5,4,8,1440]{2,1,0,3:T(4,128)(2,1)} copy(bf16[5,4,8,1440]{3,2,1,0:T(8,128)(2,1)} %fusion.28) | data formatting | bytes 921600 | tf_op jit(solution)/shard_map/convert_element_type | solution.py:116
  478.7 9.8 %reshape.277 = bf16[8,2,14400]{2,1,0:T(2,128)(2,1)S(1)} reshape(bf16[1440,5,4,8]{3,2,1,0:T(4,128)(2,1)} %bitcast.100) | data formatting | bytes 921600
  488.6 15.2 %all_to_all.97 = bf16[8,2,14400]{2,1,0:T(2,128)(2,1)S(1)} all-to-all(bf16[8,2,14400]{2,1,0:T(2,128)(2,1)S(1)} %reshape.277), channel_id=1, replica_groups=mesh['mem'=8,'tile'=16] {'mem'}, dimensions={0} | all-to-all | bytes 921600 | tf_op jit(solution)/shard_map/all_to_all | solution.py:117
  503.7 7.5 %reshape.278 = bf16[1440,5,4,8]{3,2,1,0:T(4,128)(2,1)} reshape(bf16[8,2,14400]{2,1,0:T(2,128)(2,1)S(1)} %all_to_all.97) | data formatting | bytes 921600
  511.2 8.6 %copy.110 = bf16[5,4,8,1440]{3,2,1,0:T(8,128)(2,1)S(1)} copy(bf16[5,4,8,1440]{2,1,0,3:T(4,128)(2,1)} %bitcast.101) | data formatting | bytes 921600 | tf_op jit(solution)/shard_map/all_to_all | solution.py:117
  527.0 11.8 %gather_fusion.2 = f32[2048]{0:T(1024)S(1)} fusion(f32[5760]{0:T(1024)S(1)} %mul.456, s32[2048]{0:T(1024)S(1)} %broadcast_clamp_fusion), kind=kCustom, calls=%fused_computation.2 | custom fusion | bytes 24576 | tf_op jit(solution)/shard_map/gather | solution.py:121
  538.8 22.9 %all_to_all.98 = f32[128,1,16]{2,1,0:T(1,128)S(1)} all-to-all(f32[128,1,16]{2,1,0:T(1,128)S(1)} %bitcast.129), channel_id=1, replica_groups=mesh['mem'=8,'tile'=16] {'mem','tile'}, dimensions={0} | all-to-all | bytes 16384 | tf_op jit(solution)/shard_map/all_to_all | solution.py:122
  561.7 7.1 gather_fusion.3
  568.9 4.4 scatter_custom_fusion.4
  573.5 13.9 %all_to_all.99 = f32[128,1,16]{2,1,0:T(1,128)S(1)} all-to-all(f32[128,1,16]{2,1,0:T(1,128)S(1)} %copy.114), channel_id=1, replica_groups=mesh['mem'=8,'tile'=16] {'mem','tile'}, dimensions={0} | all-to-all | bytes 16384 | tf_op jit(solution)/shard_map/all_to_all | solution.py:126
  588.3 12.9 %scatter_custom_fusion.1 = f32[5760]{0:T(1024)S(1)} fusion(s32[2048]{0:T(1024)} %bitcast.137, f32[2048]{0:T(1024)S(1)} %reshape.216, f32[]{:T(128)} %constant.17.clone.1), kind=kCustom, calls=%fused_computation.202 | custom fusion | flops 2048 | bytes 23552 | tf_op jit(solution)/shard_map/scatter-add | solution.py:130
  601.5 14.2 %all_to_all.100 = bf16[40,4,8,180]{3,2,1,0:T(8,128)(2,1)S(1)} all-to-all(bf16[40,4,8,180]{3,2,1,0:T(8,128)(2,1)S(1)} %fusion.19), channel_id=1, replica_groups=mesh['mem'=8,'tile'=16] {'mem'}, dimensions={0} | all-to-all | bytes 921600 | tf_op jit(solution)/shard_map/all_to_all | solution.py:134
  639.3 4.7 collective-permute-start.31
  657.6 36.3 %psum.62 = f32[]{:T(128)} all-reduce(f32[]{:T(128)} %get-tuple-element.6), channel_id=1, replica_groups=mesh['mem'=8,'tile'=16] {'tile'}, use_global_device_ids=true, to_apply=%region_22.23 | all-reduce | flops 1 | bytes 8 | tf_op jit(solution)/shard_map/psum | solution.py:112
  694.0 25.4 %psum.63 = f32[]{:T(128)} all-reduce(f32[]{:T(128)} %psum.62), channel_id=1, replica_groups=mesh['mem'=8,'tile'=16] {'mem'}, use_global_device_ids=true, to_apply=%region_23.24 | all-reduce | flops 1 | bytes 8 | tf_op jit(solution)/shard_map/psum | solution.py:112
  (324 shorter events, 160.8 us)
Async XLA Ops:
  2.0 24.2 %copy-start.11 = (f32[8,1440]{1,0:T(8,128)S(1)}, f32[8,1440]{1,0:T(8,128)}, u32[]{:S(2)}) copy-start(f32[8,1440]{1,0:T(8,128)} %param.18) | copy-start | bytes 138244
  2.0 24.2 %copy-start.12 = (f32[8,1440]{1,0:T(8,128)S(1)}, f32[8,1440]{1,0:T(8,128)}, u32[]{:S(2)}) copy-start(f32[8,1440]{1,0:T(8,128)} %param.17) | copy-start | bytes 138244
  2.0 29.5 %copy-start.35 = (s32[4]{0:T(128)S(1)}, s32[4]{0:T(128)}, u32[]{:S(2)}) copy-start(s32[4]{0:T(128)} %param.20) | copy-start | bytes 52
  7.7 54.1 %all-to-all-start.1 = ((s32[128,1,16]{2,1,0:T(1,128)}), s32[128,1,16]{2,1,0:T(1,128)S(1)}, u32[]{:S(2)}, u32[]{:S(2)}) async-start(s32[128,1,16]{2,1,0:T(1,128)} %copy.101), calls=%async_computation.1 | async-start | bytes 131072 | tf_op jit(solution)/shard_map/all_to_all | solution.py:106
  19.4 30.7 %copy-start.1 = (f32[5,4,8,1440]{3,2,1,0:T(8,128)}, f32[5,4,8,1440]{3,2,1,0:T(8,128)S(1)}, u32[]{:S(2)}) copy-start(f32[5,4,8,1440]{3,2,1,0:T(8,128)S(1)} %broadcast_multiply_fusion.3) | copy-start | bytes 2764804
  20.2 51.9 %collective-permute-start.2 = (f32[5,4,1,1440]{3,2,1,0:T(1,128)}, f32[5,4,1,1440]{3,2,1,0:T(1,128)}, u32[]{:S(2)}, u32[]{:S(2)}) collective-permute-start(f32[5,4,1,1440]{3,2,1,0:T(1,128)} %get-tuple-element.45), channel_id=1, source_target_pairs={{1,0},{2,1},{3,2},{4,3},{5,4},{6,5},{7,6},{8,7},{9,8},{10,9},{11,1... | collective-permute-start | bytes 345608 | tf_op jit(solution)/shard_map/ppermute | solution.py:21
  21.5 50.6 %collective-permute-start.3 = (f32[5,4,1,1440]{3,2,1,0:T(1,128)}, f32[5,4,1,1440]{3,2,1,0:T(1,128)}, u32[]{:S(2)}, u32[]{:S(2)}) collective-permute-start(f32[5,4,1,1440]{3,2,1,0:T(1,128)} %get-tuple-element.44), channel_id=1, source_target_pairs={{0,1},{1,2},{2,3},{3,4},{4,5},{5,6},{6,7},{7,8},{8,9},{9,10},{10,1... | collective-permute-start | bytes 345608 | tf_op jit(solution)/shard_map/ppermute | solution.py:18
  26.2 43.5 %collective-permute-start.1 = (f32[3,1,1440]{2,1,0:T(1,128)S(1)}, f32[3,1,1440]{2,1,0:T(1,128)S(1)}, u32[]{:S(2)}, u32[]{:S(2)}) collective-permute-start(f32[3,1,1440]{2,1,0:T(1,128)S(1)} %get-tuple-element.49), channel_id=1, source_target_pairs={{1,0},{2,1},{3,2},{4,3},{5,4},{6,5},{7,6},{8,7},{9,8},{10,9},{11,1... | collective-permute-start | bytes 51848 | tf_op jit(solution)/shard_map/ppermute | solution.py:21
  27.5 42.2 %collective-permute-start = (f32[3,1,1440]{2,1,0:T(1,128)S(1)}, f32[3,1,1440]{2,1,0:T(1,128)S(1)}, u32[]{:S(2)}, u32[]{:S(2)}) collective-permute-start(f32[3,1,1440]{2,1,0:T(1,128)S(1)} %get-tuple-element.48), channel_id=1, source_target_pairs={{0,1},{1,2},{2,3},{3,4},{4,5},{5,6},{6,7},{7,8},{8,9},{9,10},{10,1... | collective-permute-start | bytes 51848 | tf_op jit(solution)/shard_map/ppermute | solution.py:18
  32.1 41.5 %copy-start.28 = (pred[4]{0:T(512)(128)(4,1)}, pred[4]{0:T(512)(128)(4,1)S(1)}, u32[]{:S(2)}) copy-start(pred[4]{0:T(512)(128)(4,1)S(1)} %get-tuple-element.61) | copy-start | bytes 16
  32.1 70.5 %copy-start.19 = (pred[4]{0:T(512)(128)(4,1)}, pred[4]{0:T(512)(128)(4,1)S(1)}, u32[]{:S(2)}) copy-start(pred[4]{0:T(512)(128)(4,1)S(1)} %get-tuple-element.59) | copy-start | bytes 16
  61.9 58.9 %all-to-all-start = ((bf16[8,2,14400]{2,1,0:T(2,128)(2,1)}), bf16[8,2,14400]{2,1,0:T(2,128)(2,1)}, u32[]{:S(2)}, u32[]{:S(2)}) async-start(bf16[8,2,14400]{2,1,0:T(2,128)(2,1)} %reshape.273), calls=%async_computation | async-start | bytes 925696 | tf_op jit(solution)/shard_map/all_to_all | solution.py:109
  74.7 6.6 collective-permute-start.4
  76.0 6.2 collective-permute-start.5
  83.7 6.4 collective-permute-start.6
  85.0 6.6 collective-permute-start.7
  93.1 7.7 %collective-permute-start.8 = (f32[5,4,1,1440]{3,2,1,0:T(1,128)S(1)}, f32[5,4,1,1440]{3,2,1,0:T(1,128)S(1)}, u32[]{:S(2)}, u32[]{:S(2)}) collective-permute-start(f32[5,4,1,1440]{3,2,1,0:T(1,128)S(1)} %get-tuple-element.39), channel_id=1, source_target_pairs={{1,0},{2,1},{3,2},{4,3},{5,4},{6,5},{7,6},{8,7},{9,8},{10,9},{11,1... | collective-permute-start | bytes 345608 | tf_op jit(solution)/shard_map/ppermute | solution.py:21
  94.4 7.8 %collective-permute-start.9 = (f32[5,4,1,1440]{3,2,1,0:T(1,128)S(1)}, f32[5,4,1,1440]{3,2,1,0:T(1,128)S(1)}, u32[]{:S(2)}, u32[]{:S(2)}) collective-permute-start(f32[5,4,1,1440]{3,2,1,0:T(1,128)S(1)} %get-tuple-element.38), channel_id=1, source_target_pairs={{0,1},{1,2},{2,3},{3,4},{4,5},{5,6},{6,7},{7,8},{8,9},{9,10},{10,1... | collective-permute-start | bytes 345608 | tf_op jit(solution)/shard_map/ppermute | solution.py:18
  120.8 28.6 %all-to-all-start.2 = ((bf16[8,2,14400]{2,1,0:T(2,128)(2,1)}), bf16[8,2,14400]{2,1,0:T(2,128)(2,1)S(1)}, u32[]{:S(2)}, u32[]{:S(2)}) async-start(bf16[8,2,14400]{2,1,0:T(2,128)(2,1)} %reshape.275), calls=%async_computation.2 | async-start | bytes 925696 | tf_op jit(solution)/shard_map/all_to_all | solution.py:117
  149.4 79.8 %copy-start.6 = (bf16[5,4,8,1440]{3,2,1,0:T(8,128)(2,1)}, bf16[5,4,8,1440]{3,2,1,0:T(8,128)(2,1)S(1)}, u32[]{:S(2)}) copy-start(bf16[5,4,8,1440]{3,2,1,0:T(8,128)(2,1)S(1)} %copy.97) | copy-start | bytes 1382404
  224.4 14.6 %all-to-all-start.4 = ((f32[128,1,16]{2,1,0:T(1,128)}), f32[128,1,16]{2,1,0:T(1,128)S(1)}, u32[]{:S(2)}, u32[]{:S(2)}) async-start(f32[128,1,16]{2,1,0:T(1,128)} %copy.107), calls=%async_computation.4 | async-start | bytes 131072 | tf_op jit(solution)/shard_map/all_to_all | solution.py:126
  232.9 28.0 %copy-start.9 = (f32[5,4,8,1440]{3,2,1,0:T(8,128)S(1)}, f32[5,4,8,1440]{3,2,1,0:T(8,128)}, u32[]{:S(2)}) copy-start(f32[5,4,8,1440]{3,2,1,0:T(8,128)} %param.14) | copy-start | bytes 2764804
  255.9 15.9 %all-to-all-start.5 = ((bf16[40,4,8,180]{3,2,1,0:T(8,128)(2,1)}), bf16[40,4,8,180]{3,2,1,0:T(8,128)(2,1)}, u32[]{:S(2)}, u32[]{:S(2)}) async-start(bf16[40,4,8,180]{3,2,1,0:T(8,128)(2,1)} %fusion.17), calls=%async_computation.5 | async-start | bytes 1310720 | tf_op jit(solution)/shard_map/all_to_all | solution.py:134
  277.4 5.6 collective-permute-start.10
  278.7 5.8 collective-permute-start.11
  286.2 6.0 collective-permute-start.12
  287.5 6.3 collective-permute-start.13
  295.2 6.3 collective-permute-start.14
  296.5 6.5 collective-permute-start.15
  304.6 6.0 collective-permute-start.16
  305.9 6.3 collective-permute-start.17
  380.5 51.6 %copy-start.4 = (f32[5,4,8,1440]{3,2,1,0:T(8,128)}, f32[5,4,8,1440]{3,2,1,0:T(8,128)S(1)}, u32[]{:S(2)}) copy-start(f32[5,4,8,1440]{3,2,1,0:T(8,128)S(1)} %get-tuple-element.11) | copy-start | bytes 2764804
  432.6 6.7 collective-permute-start.18
  433.9 6.1 collective-permute-start.19
  441.5 6.5 collective-permute-start.20
  442.8 6.8 collective-permute-start.21
  451.0 6.3 collective-permute-start.22
  452.3 6.5 collective-permute-start.23
  460.3 6.3 collective-permute-start.24
  461.6 6.5 collective-permute-start.25
  620.3 5.6 collective-permute-start.26
  621.6 5.8 collective-permute-start.27
  629.0 6.0 collective-permute-start.28
  630.3 6.3 collective-permute-start.29
  638.0 6.3 collective-permute-start.30
  639.3 6.5 collective-permute-start.31
  647.4 6.0 collective-permute-start.32
  648.7 6.3 collective-permute-start.33
  (30 other events, 134.4 us)
